TPU v7x, 128 devices: a whole 4x4x4 slice. The times are simulated.
128 devices in a mesh: seq: 16 (over x_lo, y, core), tp: 8 (over z, x_hi).
Axes of the slice: x: 4 (x_hi: 2, x_lo: 2; x = x_hi * 2 + x_lo), y: 4, z: 4, core: 2. Of those that a mesh axis runs over, the one named last changes fastest.
Arguments:
- selected_hidden: bfloat16 [32, 104, 2048], P('seq', None, 'tp'), may hold values from -6 to 6
- cached_keys: bfloat16 [32, 1024, 1024], P('seq', None, 'tp'), may hold values from -48 to 48
- cached_values: bfloat16 [32, 1024, 1024], P('seq', None, 'tp'), may hold values from -6 to 6
- slot_spans: int32 [32], replicated, may hold values from 0 to 31, each once
- span_order: int32 [4, 8], replicated, may hold values from 0 to 7, each once within a row
- cache_start: int32 [4, 8], replicated, may hold values from 0 to 16383
- selected_index: int32 [32, 104], replicated, may hold values from 0 to 1023, as said below
- input_gain: bfloat16 [2048], replicated, may hold values from 0.5 to 2
- query_weight: bfloat16 [2048, 2048], P(None, 'tp'), may hold values from -0.125 to 0.125
- key_weight: bfloat16 [2048, 1024], P(None, 'tp'), may hold values from -0.125 to 0.125
- value_weight: bfloat16 [2048, 1024], P(None, 'tp'), may hold values from -0.125 to 0.125
- query_gain: bfloat16 [128], replicated, may hold values from 1 to 2
- key_gain: bfloat16 [128], replicated, may hold values from 1 to 2
- output_weight: bfloat16 [2048, 2048], P('tp'), may hold values from -0.125 to 0.125
- post_gain: bfloat16 [2048], replicated, may hold values from 0.5 to 2
- gate_weight: bfloat16 [2048, 6144], P(None, 'tp'), may hold values from -0.125 to 0.125
- up_weight: bfloat16 [2048, 6144], P(None, 'tp'), may hold values from -0.125 to 0.125
- down_weight: bfloat16 [6144, 2048], P('tp'), may hold values from -0.078125 to 0.078125
Outputs:
- new_hidden: bfloat16 [32, 104, 2048], P('seq', None, 'tp')
Inputs may be any that keep to these rules, and one draw needn't show every extreme that they name: `selected_index`: each row holds 104 distinct positions in increasing order. `slot_spans`: each span of each request is held by exactly one slot. `span_order`: each row places the 8 spans of a request in some order.
All inputs are finite; a program needn't handle non-finite values.
Results may differ from a plain program's by a relative error of at most 0.027.
Values may be sent and summed in bfloat16 or wider, within the bound.
No kernel may reach another device: no remote copies, remote signals or barrier semaphores. Data moves between devices by JAX's collectives and lax.ppermute only.
A program may use at most 128 MiB of HBM per device.

v0:
```python
import jax
import jax.numpy as jnp
from jax import lax
from jax.sharding import PartitionSpec as P

theta_base = 1000000.0
norm_eps = 1e-06


def rms_scale(values):
    return values * lax.rsqrt(jnp.mean(values * values, axis=-1, keepdims=True) + norm_eps)


def rotary(values, positions):
    half_len = values.shape[-1] // 2
    frequency = jnp.exp(
        -jnp.log(theta_base) * jnp.arange(half_len, dtype=jnp.float32) * 2.0 / values.shape[-1]
    )
    angles = positions.astype(jnp.float32)[..., None] * frequency
    cosine = jnp.cos(angles)[..., None, :]
    sine_part = jnp.sin(angles)[..., None, :]
    lower_half = values[..., :half_len]
    upper_half = values[..., half_len:]
    return jnp.concatenate(
        [
            lower_half * cosine - upper_half * sine_part,
            upper_half * cosine + lower_half * sine_part,
        ],
        axis=-1,
    )


def slot_table(slot_ids, slot_spans, span_order, cache_start, span_len):
    slot_count = slot_spans.shape[0]
    span_count = span_order.shape[1]
    slot_match = (slot_ids[:, None] == jnp.arange(slot_count, dtype=jnp.int32)[None, :]).astype(
        jnp.int32
    )
    span_ids = jnp.sum(slot_match * slot_spans[None, :], axis=1)
    span_match = (
        span_ids[:, None] == jnp.arange(span_order.size, dtype=jnp.int32)[None, :]
    ).astype(jnp.int32)
    new_place = jnp.sum(span_match * span_order.reshape(-1)[None, :], axis=1)
    old_start = jnp.sum(span_match * cache_start.reshape(-1)[None, :], axis=1)
    return (span_ids // span_count, new_place * span_len, old_start)


def on_device(
    selected_hidden,
    cached_keys,
    cached_values,
    slot_spans,
    span_order,
    cache_start,
    selected_index,
    input_gain,
    query_weight,
    key_weight,
    value_weight,
    query_gain,
    key_gain,
    output_weight,
    post_gain,
    gate_weight,
    up_weight,
    down_weight,
):
    slot_local, select_count, width_local = selected_hidden.shape
    span_len = cached_keys.shape[1]
    head_dim = query_gain.shape[0]
    kv_local = cached_keys.shape[2] // head_dim
    query_local = query_weight.shape[1] // head_dim
    group_size = query_local // kv_local
    row_count = slot_local * select_count
    score_scale = head_dim ** (-0.5)
    first_slot = lax.axis_index("seq") * slot_local
    local_slots = first_slot + jnp.arange(slot_local, dtype=jnp.int32)
    local_request, local_base, local_start = slot_table(
        local_slots, slot_spans, span_order, cache_start, span_len
    )
    local_index = lax.dynamic_slice_in_dim(selected_index, first_slot, slot_local, 0)
    query_pos = (local_base[:, None] + local_index).reshape(-1)
    query_request = jnp.broadcast_to(local_request[:, None], (slot_local, select_count)).reshape(-1)
    hidden_local = selected_hidden.reshape(row_count, width_local)
    hidden_full = lax.all_gather(hidden_local, "tp", axis=1, tiled=True)
    normed = (rms_scale(hidden_full.astype(jnp.float32)) * input_gain.astype(jnp.float32)).astype(
        jnp.bfloat16
    )
    query_proj = jnp.dot(normed, query_weight, preferred_element_type=jnp.float32).reshape(
        row_count, query_local, head_dim
    )
    queries = rotary(rms_scale(query_proj) * query_gain.astype(jnp.float32), query_pos).astype(
        jnp.bfloat16
    )
    key_proj = jnp.dot(normed, key_weight, preferred_element_type=jnp.float32).reshape(
        row_count, kv_local, head_dim
    )
    new_keys = rotary(rms_scale(key_proj) * key_gain.astype(jnp.float32), query_pos).astype(
        jnp.bfloat16
    )
    new_values = (
        jnp.dot(normed, value_weight, preferred_element_type=jnp.float32)
        .astype(jnp.bfloat16)
        .reshape(row_count, kv_local, head_dim)
    )
    shift_pos = jnp.broadcast_to((local_base - local_start)[:, None], (slot_local, span_len))
    shifted = rotary(
        cached_keys.reshape(slot_local, span_len, kv_local, head_dim).astype(jnp.float32), shift_pos
    ).astype(jnp.bfloat16)
    slot_rows = jnp.arange(slot_local, dtype=jnp.int32)[:, None]
    joined_keys = (
        shifted.at[slot_rows, local_index]
        .set(new_keys.reshape(slot_local, select_count, kv_local, head_dim))
        .reshape(slot_local, span_len, kv_local * head_dim)
    )
    joined_values = (
        cached_values.reshape(slot_local, span_len, kv_local, head_dim)
        .at[slot_rows, local_index]
        .set(new_values.reshape(slot_local, select_count, kv_local, head_dim))
        .reshape(slot_local, span_len, kv_local * head_dim)
    )

    def attend_block(state_in, query_set, key_block, value_block, slot_id):
        query_vecs, positions, requests = query_set
        key_request, key_base, unused_start = slot_table(
            slot_id[None], slot_spans, span_order, cache_start, span_len
        )
        key_pos = key_base[0] + jnp.arange(span_len, dtype=jnp.int32)
        visible = (requests[:, None] == key_request[0]) & (key_pos[None, :] <= positions[:, None])
        run_max, run_sum, run_acc = state_in
        grouped = query_vecs.reshape(-1, kv_local, group_size, head_dim)
        key_heads = key_block.reshape(span_len, kv_local, head_dim)
        value_heads = value_block.reshape(span_len, kv_local, head_dim)
        scores = (
            jnp.einsum("qkgd,lkd->qkgl", grouped, key_heads, preferred_element_type=jnp.float32)
            * score_scale
        )
        key_mask = visible[:, None, None, :]
        scores = jnp.where(key_mask, scores, -jnp.inf)
        new_max = jnp.maximum(run_max, jnp.max(scores, axis=-1))
        safe_max = jnp.where(new_max == -jnp.inf, 0.0, new_max)
        rescale = jnp.exp(run_max - safe_max)
        weights = jnp.where(key_mask, jnp.exp(scores - safe_max[..., None]), 0.0)
        new_sum = rescale * run_sum + jnp.sum(weights, axis=-1)
        new_acc = rescale[..., None] * run_acc + jnp.einsum(
            "qkgl,lkd->qkgd",
            weights.astype(jnp.bfloat16),
            value_heads,
            preferred_element_type=jnp.float32,
        )
        return (new_max, new_sum, new_acc)

    local_set = (queries, query_pos, query_request)
    piece_keys = lax.all_gather(joined_keys, "seq", axis=0, tiled=True)
    piece_values = lax.all_gather(joined_values, "seq", axis=0, tiled=True)

    def step_slot(running, slot_item):
        block_keys, block_values, offset = slot_item
        return (attend_block(running, local_set, block_keys, block_values, offset), None)

    state_out, unused_out = lax.scan(
        step_slot,
        (
            jnp.full((row_count, kv_local, group_size), -jnp.inf, jnp.float32),
            jnp.zeros((row_count, kv_local, group_size), jnp.float32),
            jnp.zeros((row_count, kv_local, group_size, head_dim), jnp.float32),
        ),
        (piece_keys, piece_values, jnp.arange(piece_keys.shape[0], dtype=jnp.int32)),
    )
    run_max, run_sum, run_acc = state_out
    attended = (run_acc / run_sum[..., None]).astype(jnp.bfloat16)
    out_part = jnp.dot(
        attended.reshape(row_count, query_local * head_dim),
        output_weight,
        preferred_element_type=jnp.float32,
    )
    attention_sum = lax.psum(out_part.astype(jnp.bfloat16), "tp").astype(jnp.float32)
    stream = (hidden_full.astype(jnp.float32) + attention_sum).astype(jnp.bfloat16)
    normed_post = (rms_scale(stream.astype(jnp.float32)) * post_gain.astype(jnp.float32)).astype(
        jnp.bfloat16
    )
    gate_values = jnp.dot(normed_post, gate_weight, preferred_element_type=jnp.float32)
    up_values = jnp.dot(normed_post, up_weight, preferred_element_type=jnp.float32)
    active = (jax.nn.silu(gate_values) * up_values).astype(jnp.bfloat16)
    feedforward_sum = lax.psum(
        jnp.dot(active, down_weight, preferred_element_type=jnp.float32).astype(jnp.bfloat16), "tp"
    ).astype(jnp.float32)
    result_full = (stream.astype(jnp.float32) + feedforward_sum).astype(jnp.bfloat16)
    result = lax.dynamic_slice_in_dim(
        result_full, lax.axis_index("tp") * width_local, width_local, 1
    )
    return result.reshape(slot_local, select_count, width_local)


def solution(mesh):
    in_specs = (
        P("seq", None, "tp"),
        P("seq", None, "tp"),
        P("seq", None, "tp"),
        P(),
        P(),
        P(),
        P(),
        P(),
        P(None, "tp"),
        P(None, "tp"),
        P(None, "tp"),
        P(),
        P(),
        P("tp", None),
        P(),
        P(None, "tp"),
        P(None, "tp"),
        P("tp", None),
    )
    out_specs = P("seq", None, "tp")
    return jax.shard_map(
        on_device, mesh=mesh, in_specs=in_specs, out_specs=out_specs, check_vma=False
    )
```

profile of v0, /device:TPU:0, one launch (start us, length us, event | category | flops | bytes accessed | tf_op | source)
XLA Modules:
  0.0 828.0 jit_solution(6008349107138852399)
XLA Ops:
  19.5 38.6 %all_gather.9 = bf16[208,2048]{1,0:T(8,128)(2,1)S(1)} all-gather(bf16[208,256]{1,0:T(8,128)(2,1)S(1)} %bitcast.112), channel_id=1, replica_groups=mesh['seq'=16,'tp'=8] {'tp'}, dimensions={1}, use_global_device_ids=true | all-gather | bytes 958464 | tf_op jit(solution)/shard_map/all_gather | solution.py:85
  60.4 21.8 %scatter_fusion = bf16[2,1024,128]{2,1,0:T(8,128)(2,1)} fusion(bf16[2,1024,128]{2,1,0:T(8,128)(2,1)} %copy.36, s32[208]{0:T(256)S(1)} %reshape.474, bf16[208,128]{1,0:T(8,128)(2,1)S(1)} %bitcast.111), kind=kCustom, calls=%fused_computation | custom fusion | bytes 161408 | tf_op jit(solution)/shard_map/scatter | solution.py:113
  84.0 21.9 %scatter_fusion.1 = bf16[2,1024,128]{2,1,0:T(8,128)(2,1)} fusion(bf16[2,1024,128]{2,1,0:T(8,128)(2,1)} %copy.64, s32[208]{0:T(256)S(1)} %reshape.474, bf16[208,128]{1,0:T(8,128)(2,1)S(1)} %convolution_convert_fusion.2), kind=kCustom, calls=%fused_computation.1 | custom fusion | bytes 161408 | tf_op jit(solution)/shard_map/scatter | solution.py:119
  106.0 2.6 fusion.63
  112.0 24.0 %all-gather.5.cloned.1.call-done = bf16[32,1024,128]{2,1,0:T(8,128)(2,1)} async-done(((bf16[2,1024,128]{2,1,0:T(8,128)(2,1)}), bf16[32,1024,128]{2,1,0:T(8,128)(2,1)}) %all-gather.5.cloned.1.call-update) | async-done | bytes 8388624 | tf_op jit(solution)/shard_map/all_gather | solution.py:154
  135.9 54.8 %all-gather.7.cloned.1.call-done = bf16[32,1024,128]{2,1,0:T(8,128)(2,1)} async-done(((bf16[2,1024,128]{2,1,0:T(8,128)(2,1)}), bf16[32,1024,128]{2,1,0:T(8,128)(2,1)}) %all-gather.7.cloned.1.call-update) | async-done | bytes 8388624 | tf_op jit(solution)/shard_map/all_gather | solution.py:155
  190.8 436.8 %while.18 = (s32[]{:T(128)}, f32[208,1,2]{0,2,1:T(2,128)S(1)}, f32[208,1,2]{0,2,1:T(2,128)S(1)}, f32[208,1,2,128]{3,0,2,1:T(8,128)}, s32[32]{0:T(128)S(1)}, /*in...) while((s32[]{:T(128)}, f32[208,1,2]{0,2,1:T(2,128)S(1)}, ...), condition=%wide.wide.region_13.14_spmd.clone, body=%wide.wide.region_8.13_spmd.clone.sunk | while | flops 222529680 | bytes 15580799 | solution.py:161
  211.0 2.6 fusion.101
  224.7 2.6 fusion.101
  238.3 2.6 fusion.101
  252.0 2.6 fusion.101
  265.6 2.6 fusion.101
  279.3 2.6 fusion.101
  292.9 2.6 fusion.101
  306.6 2.6 fusion.101
  320.2 2.6 fusion.101
  333.9 2.6 fusion.101
  347.5 2.6 fusion.101
  361.2 2.6 fusion.101
  374.8 2.6 fusion.101
  388.5 2.6 fusion.101
  402.1 2.6 fusion.101
  415.8 2.6 fusion.101
  429.4 2.6 fusion.101
  443.1 2.6 fusion.101
  456.7 2.6 fusion.101
  484.0 2.6 fusion.101
  631.4 89.7 %all-reduce.3.cloned.1.call-done = bf16[208,2048]{1,0:T(8,128)(2,1)} async-done(((bf16[208,2048]{1,0:T(8,128)(2,1)}), bf16[208,2048]{1,0:T(8,128)(2,1)}) %all-reduce.3.cloned.1.call-update) | async-done | bytes 851984 | tf_op jit(solution)/shard_map/psum | solution.py:177
  721.1 3.0 multiply_reduce_fusion
  724.1 3.7 fusion.58
  727.8 5.3 convolution_convert_fusion
  733.1 86.7 %all-reduce.5.cloned.1.call-done = bf16[208,2048]{1,0:T(8,128)(2,1)} async-done(((bf16[208,2048]{1,0:T(8,128)(2,1)}), bf16[208,2048]{1,0:T(8,128)(2,1)}) %all-reduce.5.cloned.1.call-update) | async-done | bytes 851984 | tf_op jit(solution)/shard_map/psum | solution.py:185
  (734 shorter events, 313.2 us)
Async XLA Ops:
  6.5 721.2 %copy-start = (bf16[768,2048]{1,0:T(8,128)(2,1)S(1)}, bf16[768,2048]{1,0:T(8,128)(2,1)}, u32[]{:S(2)}) copy-start(bf16[768,2048]{1,0:T(8,128)(2,1)} %param.37) | copy-start | bytes 9437188
  6.5 129.4 %all-gather.5.cloned.1.call-start = ((), (), s32[]{:S(2)}) async-start(), calls=%async_computation.2 | async-start | bytes 8912896 | tf_op jit(solution)/shard_map/all_gather | solution.py:154
  12.6 97.5 %copy-start.11 = (s32[2,104]{1,0:T(2,128)}, s32[2,104]{1,0:T(2,128)S(1)}, u32[]{:S(2)}) copy-start(s32[2,104]{1,0:T(2,128)S(1)} %get-tuple-element.392) | copy-start | bytes 2500
  15.8 3.7 copy-start.7
  16.5 41.6 %copy-start.9 = (bf16[2048]{0:T(1024)(128)(2,1)S(1)}, bf16[2048]{0:T(1024)(128)(2,1)}, u32[]{:S(2)}) copy-start(bf16[2048]{0:T(1024)(128)(2,1)} %param.27) | copy-start | bytes 12292
  16.5 41.9 %copy-start.13 = (bf16[128]{0:T(256)(128)(2,1)S(1)}, bf16[128]{0:T(256)(128)(2,1)}, u32[]{:S(2)}) copy-start(bf16[128]{0:T(256)(128)(2,1)} %param.32) | copy-start | bytes 772
  19.5 39.5 %copy-start.12 = (bf16[2048,128]{1,0:T(8,128)(2,1)S(1)}, bf16[2048,128]{1,0:T(8,128)(2,1)}, u32[]{:S(2)}) copy-start(bf16[2048,128]{1,0:T(8,128)(2,1)} %param.29) | copy-start | bytes 1572868
  82.2 23.8 %copy-start.14 = (bf16[128]{0:T(256)(128)(2,1)S(1)}, bf16[128]{0:T(256)(128)(2,1)}, u32[]{:S(2)}) copy-start(bf16[128]{0:T(256)(128)(2,1)} %param.31) | copy-start | bytes 772
  82.2 108.6 %all-gather.7.cloned.1.call-start = ((), (), s32[]{:S(2)}) async-start(), calls=%async_computation.3 | async-start | bytes 8912896 | tf_op jit(solution)/shard_map/all_gather | solution.py:155
  105.9 615.2 %all-reduce.3.cloned.1.call-start = ((), (), s32[]{:S(2)}) async-start(), calls=%async_computation | async-start | bytes 1703936 | tf_op jit(solution)/shard_map/psum | solution.py:177
  108.6 82.1 %copy-start.8 = (s32[4,8]{1,0:T(4,128)S(1)}, s32[4,8]{1,0:T(4,128)}, u32[]{:S(2)}) copy-start(s32[4,8]{1,0:T(4,128)} %param.24) | copy-start | bytes 388
  108.6 82.1 %copy-start.15 = (s32[32]{0:T(128)S(1)}, s32[32]{0:T(128)}, u32[]{:S(2)}) copy-start(s32[32]{0:T(128)} %param.23) | copy-start | bytes 388
  200.0 2.2 copy-start.5
  213.6 2.2 copy-start.5
  227.3 2.2 copy-start.5
  240.9 2.2 copy-start.5
  254.6 2.2 copy-start.5
  268.2 2.2 copy-start.5
  281.9 2.2 copy-start.5
  295.5 2.2 copy-start.5
  309.2 2.2 copy-start.5
  322.8 2.2 copy-start.5
  350.1 2.2 copy-start.5
  363.8 2.2 copy-start.5
  391.1 2.2 copy-start.5
  404.7 2.2 copy-start.5
  432.0 2.2 copy-start.5
  445.7 2.2 copy-start.5
  627.6 3.8 copy-start.10
  631.3 188.5 %all-reduce.5.cloned.1.call-start = ((), (), s32[]{:S(2)}) async-start(), calls=%async_computation.1 | async-start | bytes 1703936 | tf_op jit(solution)/shard_map/psum | solution.py:185
  721.1 3.0 copy-start.3
  721.1 3.0 copy-start.4
  (81 other events, 128.2 us)
Sparse Core Ops, SparseCore 0:
  82.3 53.5 all-gather.4
  137.7 53.0 all-gather.6
  631.4 89.5 all-reduce.2
  733.2 86.5 all-reduce.4
where the time goes:
time: 833 us; the launch traced here: 828 us
  waiting for transfers between devices  255 us (31%)
  other arithmetic  173 us (21%)
  matrix products  149 us (18%)
  local copies, waits for them, and re-layouts  101 us (12%)
  loops' own time  96.9 us (12%)
  blocking collectives  38.6 us (5%)
  between operations  13.4 us (2%)
    another operation x1, loops' own time, on_device(): lax.scan(step_slot, (jnp.full((row_count, kv_local, group_size), -jnp.inf...  96.9 us
    psum x1, waiting for transfers between devices, on_device(): lax.psum(out_part.astype(jnp.bfloat16), 'tp').astype(jnp.float32)  89.7 us
    psum x1, waiting for transfers between devices, on_device(): lax.psum(jnp.dot(active, down_weight, preferred_element_type=jnp.float32)...  86.7 us
    dot_general x32, matrix products, attend_block(): jnp.einsum('qkgd,lkd->qkgl', grouped, key_heads, preferred_element_type=j...  84.1 us
    reduce_sum x32, other arithmetic, attend_block(): new_sum = rescale * run_sum + jnp.sum(weights, axis=-1)  68.4 us
    all_gather x1, waiting for transfers between devices, on_device(): piece_values = lax.all_gather(joined_values, 'seq', axis=0, tiled=True)  54.8 us
    dot_general x32, matrix products, attend_block(): jnp.einsum('qkgl,lkd->qkgd', weights.astype(jnp.bfloat16), value_heads, p...  48.8 us
    reduce_sum x33, other arithmetic, slot_table(): span_ids = jnp.sum(slot_match * slot_spans[None, :], axis=1)  42.8 us
  transfers between devices with their start and end apart: 4, of which 4 were waited for; matrix products, arithmetic and copies ran while one was open for 4% of the time, Pallas kernels for 0%

commit v1 on v0

--- a/solution.py
+++ b/solution.py
@@ -82,7 +82,9 @@
     query_pos = (local_base[:, None] + local_index).reshape(-1)
     query_request = jnp.broadcast_to(local_request[:, None], (slot_local, select_count)).reshape(-1)
     hidden_local = selected_hidden.reshape(row_count, width_local)
-    hidden_full = lax.all_gather(hidden_local, "tp", axis=1, tiled=True)
+    hidden_full = jnp.concatenate(
+        lax.all_to_all(jnp.stack([hidden_local] * lax.axis_size("tp")), "tp", 0, 0), axis=1
+    )
     normed = (rms_scale(hidden_full.astype(jnp.float32)) * input_gain.astype(jnp.float32)).astype(
         jnp.bfloat16
     )

time: 833 us -> 799 us (0.959)
  blocking collectives: 38.6 us -> 0 us
    all_gather x1 -> x0, blocking collectives: 38.6 us -> none  [on_device(): hidden_full = lax.all_gather(hidden_local, 'tp', axis=1, tiled=True)]
  transfers between devices with their start and end apart: 4 -> 5, of which waited for: 4 -> 5; matrix products, arithmetic and copies ran while one was open for 4% -> 6% of each run, Pallas kernels for 0% -> 0%
where the time goes in v1:
time: 799 us; the launch traced here: 794 us
  waiting for transfers between devices  251 us (31%)
  other arithmetic  172 us (22%)
  matrix products  147 us (18%)
  local copies, waits for them, and re-layouts  104 us (13%)
  loops' own time  98.2 us (12%)
  between operations  13.4 us (2%)
  starting transfers between devices  8.2 us (1%)
    another operation x1, loops' own time, on_device(): lax.scan(step_slot, (jnp.full((row_count, kv_local, group_size), -jnp.inf...  98.2 us
    psum x1, waiting for transfers between devices, on_device(): lax.psum(out_part.astype(jnp.bfloat16), 'tp').astype(jnp.float32)  89.6 us
    psum x1, waiting for transfers between devices, on_device(): lax.psum(jnp.dot(active, down_weight, preferred_element_type=jnp.float32)...  86.7 us
    dot_general x32, matrix products, attend_block(): jnp.einsum('qkgd,lkd->qkgl', grouped, key_heads, preferred_element_type=j...  83.8 us
    reduce_sum x32, other arithmetic, attend_block(): new_sum = rescale * run_sum + jnp.sum(weights, axis=-1)  68.4 us
    all_gather x1, waiting for transfers between devices, on_device(): piece_values = lax.all_gather(joined_values, 'seq', axis=0, tiled=True)  54.8 us
    dot_general x32, matrix products, attend_block(): jnp.einsum('qkgl,lkd->qkgd', weights.astype(jnp.bfloat16), value_heads, p...  48.8 us
    reduce_sum x33, other arithmetic, slot_table(): span_ids = jnp.sum(slot_match * slot_spans[None, :], axis=1)  38.7 us
  transfers between devices with their start and end apart: 5, of which 5 were waited for; matrix products, arithmetic and copies ran while one was open for 6% of the time, Pallas kernels for 0%

profile of v1, /device:TPU:0, one launch (start us, length us, event | category | flops | bytes accessed | tf_op | source)
XLA Modules:
  0.0 794.1 jit_solution(5647591279669594033)
XLA Ops:
  10.5 7.9 all-to-all-start
  30.3 3.3 all-to-all-done
  38.4 21.7 %scatter_fusion = bf16[2,1024,128]{2,1,0:T(8,128)(2,1)} fusion(bf16[2,1024,128]{2,1,0:T(8,128)(2,1)} %copy.43, s32[208]{0:T(256)S(1)} %reshape.485, bf16[208,128]{1,0:T(8,128)(2,1)S(1)} %bitcast.118), kind=kCustom, calls=%fused_computation | custom fusion | bytes 161408 | tf_op jit(solution)/shard_map/scatter | solution.py:115
  62.2 21.7 %scatter_fusion.1 = bf16[2,1024,128]{2,1,0:T(8,128)(2,1)} fusion(bf16[2,1024,128]{2,1,0:T(8,128)(2,1)} %copy.71, s32[208]{0:T(256)S(1)} %reshape.485, bf16[208,128]{1,0:T(8,128)(2,1)S(1)} %convolution_convert_fusion.2), kind=kCustom, calls=%fused_computation.1 | custom fusion | bytes 161408 | tf_op jit(solution)/shard_map/scatter | solution.py:121
  94.2 16.8 %all-gather.5.cloned.1.call-done = bf16[32,1024,128]{2,1,0:T(8,128)(2,1)} async-done(((bf16[2,1024,128]{2,1,0:T(8,128)(2,1)}), bf16[32,1024,128]{2,1,0:T(8,128)(2,1)}) %all-gather.5.cloned.1.call-update) | async-done | bytes 8388624 | tf_op jit(solution)/shard_map/all_gather | solution.py:156
  111.1 54.8 %all-gather.7.cloned.1.call-done = bf16[32,1024,128]{2,1,0:T(8,128)(2,1)} async-done(((bf16[2,1024,128]{2,1,0:T(8,128)(2,1)}), bf16[32,1024,128]{2,1,0:T(8,128)(2,1)}) %all-gather.7.cloned.1.call-update) | async-done | bytes 8388624 | tf_op jit(solution)/shard_map/all_gather | solution.py:157
  165.9 429.4 %while.18 = (s32[]{:T(128)}, f32[208,1,2]{0,2,1:T(2,128)S(1)}, f32[208,1,2]{0,2,1:T(2,128)S(1)}, f32[208,1,2,128]{3,0,2,1:T(8,128)}, s32[32]{0:T(128)S(1)}, /*in...) while((s32[]{:T(128)}, f32[208,1,2]{0,2,1:T(2,128)S(1)}, ...), condition=%wide.wide.region_13.14_spmd.clone, body=%wide.wide.region_8.13_spmd.clone.sunk | while | flops 222529680 | bytes 15580799 | solution.py:163
  172.2 2.6 fusion.94
  199.0 2.6 fusion.94
  212.5 2.6 fusion.94
  225.9 2.6 fusion.94
  239.3 2.6 fusion.94
  252.7 2.6 fusion.94
  279.6 2.6 fusion.94
  306.4 2.6 fusion.94
  319.8 2.6 fusion.94
  333.2 2.6 fusion.94
  346.7 2.6 fusion.94
  360.1 2.6 fusion.94
  386.9 2.6 fusion.94
  413.8 2.6 fusion.94
  427.2 2.6 fusion.94
  440.6 2.6 fusion.94
  454.0 2.6 fusion.94
  467.4 2.6 fusion.94
  494.3 2.6 fusion.94
  521.1 2.6 fusion.94
  547.9 2.6 fusion.94
  574.8 2.6 fusion.94
  599.2 89.6 %all-reduce.3.cloned.1.call-done = bf16[208,2048]{1,0:T(8,128)(2,1)} async-done(((bf16[208,2048]{1,0:T(8,128)(2,1)}), bf16[208,2048]{1,0:T(8,128)(2,1)}) %all-reduce.3.cloned.1.call-update) | async-done | bytes 851984 | tf_op jit(solution)/shard_map/psum | solution.py:179
  693.9 5.3 convolution_convert_fusion
  699.2 86.7 %all-reduce.5.cloned.1.call-done = bf16[208,2048]{1,0:T(8,128)(2,1)} async-done(((bf16[208,2048]{1,0:T(8,128)(2,1)}), bf16[208,2048]{1,0:T(8,128)(2,1)}) %all-reduce.5.cloned.1.call-update) | async-done | bytes 851984 | tf_op jit(solution)/shard_map/psum | solution.py:187
  (740 shorter events, 317.2 us)
Async XLA Ops:
  6.5 687.3 %copy-start = (bf16[768,2048]{1,0:T(8,128)(2,1)S(1)}, bf16[768,2048]{1,0:T(8,128)(2,1)}, u32[]{:S(2)}) copy-start(bf16[768,2048]{1,0:T(8,128)(2,1)} %param.37) | copy-start | bytes 9437188
  6.5 12.0 %copy-start.8 = (s32[4,8]{1,0:T(4,128)S(1)}, s32[4,8]{1,0:T(4,128)}, u32[]{:S(2)}) copy-start(s32[4,8]{1,0:T(4,128)} %param.24) | copy-start | bytes 388
  6.5 11.9 %copy-start.12 = (s32[4,8]{1,0:T(4,128)S(1)}, s32[4,8]{1,0:T(4,128)}, u32[]{:S(2)}) copy-start(s32[4,8]{1,0:T(4,128)} %param.25) | copy-start | bytes 388
  10.5 23.1 %all-to-all-start = ((bf16[8,208,256]{2,1,0:T(8,128)(2,1)}), bf16[8,208,256]{2,1,0:T(8,128)(2,1)}, u32[]{:S(2)}, u32[]{:S(2)}) async-start(bf16[8,208,256]{2,1,0:T(8,128)(2,1)} %stack.3), calls=%async_computation | async-start | bytes 1703936 | tf_op jit(solution)/shard_map/all_to_all | solution.py:86
  18.3 4.5 copy-start.15
  18.3 92.7 %all-gather.5.cloned.1.call-start = ((), (), s32[]{:S(2)}) async-start(), calls=%async_computation.3 | async-start | bytes 8912896 | tf_op jit(solution)/shard_map/all_gather | solution.py:156
  23.2 6.2 copy-start.9
  23.2 6.2 copy-start.13
  30.2 56.1 %copy-start.11 = (s32[2,104]{1,0:T(2,128)}, s32[2,104]{1,0:T(2,128)S(1)}, u32[]{:S(2)}) copy-start(s32[2,104]{1,0:T(2,128)S(1)} %get-tuple-element.394) | copy-start | bytes 2500
  34.9 2.3 copy-start.5
  35.1 2.7 copy-start.2
  60.1 105.7 %all-gather.7.cloned.1.call-start = ((), (), s32[]{:S(2)}) async-start(), calls=%async_computation.4 | async-start | bytes 8912896 | tf_op jit(solution)/shard_map/all_gather | solution.py:157
  62.1 24.1 %copy-start.14 = (bf16[128]{0:T(256)(128)(2,1)S(1)}, bf16[128]{0:T(256)(128)(2,1)}, u32[]{:S(2)}) copy-start(bf16[128]{0:T(256)(128)(2,1)} %param.31) | copy-start | bytes 772
  83.9 604.9 %all-reduce.3.cloned.1.call-start = ((), (), s32[]{:S(2)}) async-start(), calls=%async_computation.1 | async-start | bytes 1703936 | tf_op jit(solution)/shard_map/psum | solution.py:179
  188.2 2.2 copy-start.6
  201.7 2.2 copy-start.6
  215.1 2.2 copy-start.6
  228.5 2.2 copy-start.6
  241.9 2.2 copy-start.6
  255.3 2.2 copy-start.6
  268.8 2.2 copy-start.6
  295.6 2.2 copy-start.6
  309.0 2.2 copy-start.6
  322.4 2.2 copy-start.6
  335.9 2.2 copy-start.6
  349.3 2.2 copy-start.6
  362.7 2.2 copy-start.6
  376.1 2.2 copy-start.6
  389.5 2.2 copy-start.6
  595.3 4.0 copy-start.10
  599.0 186.9 %all-reduce.5.cloned.1.call-start = ((), (), s32[]{:S(2)}) async-start(), calls=%async_computation.2 | async-start | bytes 1703936 | tf_op jit(solution)/shard_map/psum | solution.py:187
  688.8 3.3 copy-start.4
  (82 other events, 131.2 us)
Sparse Core Ops, SparseCore 0:
  60.2 50.7 all-gather.4
  112.8 53.0 all-gather.6
  599.1 89.6 all-reduce.2
  699.3 86.5 all-reduce.4
